TPU v7x, 128 devices: a whole 4x4x4 slice. The times are simulated.
128 devices in a mesh: modes: 16 (over z_lo, y, core), tiles: 8 (over z_hi, x).
Axes of the slice: x: 4, y: 4, z: 4 (z_hi: 2, z_lo: 2; z = z_hi * 2 + z_lo), core: 2. Of those that a mesh axis runs over, the one named last changes fastest.
Arguments:
- solution_modes: float32 [512, 32, 8, 128], P('modes', 'tiles'), may hold values from -6 to 6
- coefficient_modes: float32 [128, 32, 8, 128], P('modes', 'tiles'), may hold values from 0.5 to 4
- coupling: float32 [16, 32, 32, 32], P('modes'), may hold values from -0.03125 to 0.03125
- source_block: int32 [16, 32], P('modes'), may hold values from 0 to 15
- expansion_index: int32 [16, 32], P('modes'), may hold values from 0 to 127
Outputs:
- applied: float32 [512, 32, 8, 128], P('modes', 'tiles')
All inputs are finite; a program needn't handle non-finite values.
Results may differ from a plain program's by a relative error of at most 0.0003.
Values sent between devices are 32-bit elements; how exact they have to be, the bound alone decides.
A program may use at most 128 MiB of HBM per device.

v0:
```python
import jax
import jax.numpy as jnp
from jax import lax
from jax.sharding import PartitionSpec as P


def with_halo(value, sides, width):
    for axis, dim in sides:
        count, length = (lax.axis_size(axis), value.shape[dim])
        up = [(i, (i + 1) % count) for i in range(count - 1)]
        down = [(j, i) for i, j in up]
        last = lax.slice_in_dim(value, length - width, length, axis=dim)
        initial = lax.slice_in_dim(value, 0, width, axis=dim)
        before = lax.ppermute(last, axis, up)
        after = lax.ppermute(initial, axis, down)
        value = jnp.concatenate([before, value, after], axis=dim)
    return value


def face_means(coefficient):
    along_first = 0.5 * (coefficient[:, :-1, 1:-1, 1:-1] + coefficient[:, 1:, 1:-1, 1:-1])
    along_second = 0.5 * (coefficient[:, 1:-1, :-1, 1:-1] + coefficient[:, 1:-1, 1:, 1:-1])
    along_third = 0.5 * (coefficient[:, 1:-1, 1:-1, :-1] + coefficient[:, 1:-1, 1:-1, 1:])
    return (along_first, along_second, along_third)


def divergence(blended, along_first, along_second, along_third):
    flux_first = along_first * (blended[:, :-1, 1:-1, 1:-1] - blended[:, 1:, 1:-1, 1:-1])
    flux_second = along_second * (blended[:, 1:-1, :-1, 1:-1] - blended[:, 1:-1, 1:, 1:-1])
    flux_third = along_third * (blended[:, 1:-1, 1:-1, :-1] - blended[:, 1:-1, 1:-1, 1:])
    result = flux_first[:, 1:] - flux_first[:, :-1]
    result = result + flux_second[:, :, 1:] - flux_second[:, :, :-1]
    return result + flux_third[:, :, :, 1:] - flux_third[:, :, :, :-1]


def slot_term(padded_u, faces, block_matrix, offset, expansion, width):
    first_faces, second_faces, third_faces = faces
    source_modes = lax.dynamic_slice_in_dim(padded_u, offset * width, width, 0)
    blended = jnp.einsum(
        "ij,jxyz->ixyz", block_matrix, source_modes, precision=lax.Precision.HIGHEST
    )
    return divergence(
        blended,
        lax.dynamic_index_in_dim(first_faces, expansion, 0, keepdims=False),
        lax.dynamic_index_in_dim(second_faces, expansion, 0, keepdims=False),
        lax.dynamic_index_in_dim(third_faces, expansion, 0, keepdims=False),
    )


def block_output(padded_u, faces, coupling_rows, source_rows, expansion_rows, width):
    shape = (width, padded_u.shape[1] - 2, padded_u.shape[2] - 2, padded_u.shape[3] - 2)

    def advance(running, slot_index):
        source = source_rows[slot_index]
        expansion = expansion_rows[slot_index]
        term = slot_term(padded_u, faces, coupling_rows[slot_index], source, expansion, width)
        return (running + term, None)

    start = jnp.zeros(shape, jnp.float32)
    total, _ = lax.scan(advance, start, jnp.arange(source_rows.shape[0], dtype=jnp.int32))
    return total


def on_device(solution_modes, coefficient_modes, coupling, source_block, expansion_index):
    local_solution = solution_modes.shape[0]
    local_coefficient = coefficient_modes.shape[0]
    width = coupling.shape[2]
    groups = lax.axis_size("modes")
    padding = ((0, 0), (0, 0), (1, 1), (1, 1))
    stacked = jnp.concatenate([solution_modes, coefficient_modes], axis=0)
    rimmed = with_halo(stacked, (("tiles", 1),), 1)
    everyone = lax.all_gather(rimmed, "modes", axis=0, tiled=True)
    trailing = everyone.shape[1:]
    shaped = everyone.reshape((groups, local_solution + local_coefficient) + trailing)
    all_solution = shaped[:, :local_solution].reshape((groups * local_solution,) + trailing)
    all_coefficient = shaped[:, local_solution:].reshape((groups * local_coefficient,) + trailing)
    padded_u = jnp.pad(all_solution, padding)
    padded_a = jnp.pad(all_coefficient, padding)
    faces = face_means(padded_a)
    outputs = block_output(padded_u, faces, coupling[0], source_block[0], expansion_index[0], width)
    return outputs


def solution(mesh):
    placed = (
        P("modes", "tiles", None, None),
        P("modes", "tiles", None, None),
        P("modes", None, None, None),
        P("modes", None),
        P("modes", None),
    )
    return jax.shard_map(
        on_device,
        mesh=mesh,
        in_specs=placed,
        out_specs=P("modes", "tiles", None, None),
        check_vma=False,
    )
```

profile of v0, /device:TPU:1, one launch (start us, length us, event | category | flops | bytes accessed | tf_op | source)
XLA Modules:
  0.0 699.4 jit_solution(3090703868489263197)
XLA Ops:
  9.9 4.6 collective-permute-start
  17.7 95.7 %all-gather.2.cloned.1.call-done = f32[640,6,8,128]{3,2,1,0:T(8,128)} async-done(((f32[40,6,8,128]{3,2,1,0:T(8,128)}), f32[640,6,8,128]{3,2,1,0:T(8,128)}) %all-gather.2.cloned.1.call-update) | async-done | bytes 15728656 | tf_op jit(solution)/shard_map/all_gather | solution.py:72
  115.6 10.5 %slice.107 = f32[16,32,6,8,128]{4,3,2,1,0:T(8,128)} slice(f32[16,40,6,8,128]{4,3,2,1,0:T(8,128)} %bitcast.41), slice={[0:16], [0:32], [0:6], [0:8], [0:128]} | slice | bytes 25165824 | tf_op jit(solution)/shard_map/slice | solution.py:75
  133.7 13.2 %copy.8 = f32[16,32,6,8,128]{4,1,0,3,2:T(8,128)} copy(f32[16,32,6,8,128]{4,3,2,1,0:T(8,128)} %slice.107) | data formatting | bytes 25165824 | tf_op jit(solution)/shard_map/slice | solution.py:75
  146.9 15.0 %pad.8 = f32[512,6,10,130]{3,0,2,1:T(8,128)} pad(f32[512,6,8,128]{3,0,2,1:T(8,128)} %bitcast.39, f32[]{:T(128)} %constant.32.clone.1), padding=0_0x0_0x1_1x1_1 | pad | bytes 28557316 | tf_op jit(solution)/shard_map/jit(_pad)/pad | solution.py:77
  162.0 528.5 %while.11 = (s32[]{:T(128)}, f32[32,4,8,128]{3,0,2,1:T(8,128)}, s32[32]{0:T(128)S(1)}, s32[32]{0:T(128)S(1)}, f32[128,5,8,128]{3,2,1,0:T(8,128)}, /*index=5*/f32...) while((s32[]{:T(128)}, f32[32,4,8,128]{3,0,2,1:T(8,128)}, ...), condition=%wide.region_1.2_spmd.clone, body=%wide.region_0.1_spmd.clone.sunk | while | flops 97650696 | bytes 12662481 | solution.py:60
  165.7 3.3 fusion.24
  182.1 3.3 fusion.24
  198.6 3.3 fusion.24
  231.6 3.3 fusion.24
  264.7 3.3 fusion.24
  297.7 3.3 fusion.24
  330.7 3.3 fusion.24
  347.3 3.3 fusion.24
  380.3 3.3 fusion.24
  413.3 3.3 fusion.24
  479.4 3.3 fusion.24
  495.9 3.3 fusion.24
  529.0 3.3 fusion.24
  562.0 3.3 fusion.24
  595.0 3.3 fusion.24
  611.6 3.3 fusion.24
  628.1 3.3 fusion.24
  677.6 3.3 fusion.24
  (354 shorter events, 349.2 us)
Async XLA Ops:
  6.5 106.9 %all-gather.2.cloned.1.call-start = ((), (), s32[]{:S(2)}) async-start(), calls=%async_computation | async-start | bytes 16711680 | tf_op jit(solution)/shard_map/all_gather | solution.py:72
  8.6 7.4 %collective-permute-start.1 = (f32[40,1,8,128]{3,2,1,0:T(8,128)S(1)}, f32[40,1,8,128]{3,2,1,0:T(8,128)S(1)}, u32[]{:S(2)}, u32[]{:S(2)}) collective-permute-start(f32[40,1,8,128]{3,2,1,0:T(8,128)S(1)} %get-tuple-element.112), channel_id=1, source_target_pairs={{1,0},{2,1},{3,2},{4,3},{5,4},{6,5},{7,6},{9,8},{10,9},{11,10},{12... | collective-permute-start | bytes 491528 | tf_op jit(solution)/shard_map/ppermute | solution.py:15
  9.9 6.8 collective-permute-start
  146.9 15.0 %copy-start = (s32[1,32]{1,0:T(1,128)S(1)}, s32[1,32]{1,0:T(1,128)}, u32[]{:S(2)}) copy-start(s32[1,32]{1,0:T(1,128)} %param.11) | copy-start | bytes 388
  146.9 15.0 %copy-start.1 = (s32[1,32]{1,0:T(1,128)S(1)}, s32[1,32]{1,0:T(1,128)}, u32[]{:S(2)}) copy-start(s32[1,32]{1,0:T(1,128)} %param.10) | copy-start | bytes 388
Sparse Core Ops, SparseCore 0:
  17.8 95.5 all-gather.1
where the time goes:
time: 710 us; the launch traced here: 699 us
  local copies, waits for them, and re-layouts  177 us (25%)
  other arithmetic  161 us (23%)
  loops' own time  138 us (19%)
  matrix products  106 us (15%)
  waiting for transfers between devices  97.9 us (14%)
  between operations  13.4 us (2%)
    another operation x1, loops' own time, block_output(): lax.scan(advance, start, jnp.arange(source_rows.shape[0], dtype=jnp.int32))  138 us
    dot_general x32, matrix products, slot_term(): jnp.einsum('ij,jxyz->ixyz', block_matrix, source_modes, precision=lax.Pre...  106 us
    all_gather x1, waiting for transfers between devices, on_device(): everyone = lax.all_gather(rimmed, 'modes', axis=0, tiled=True)  95.7 us
    add x32, other arithmetic, advance(): return (running + term, None)  84.6 us
    mul x32, other arithmetic, divergence(): along_third * (blended[:, 1:-1, 1:-1, :-1] - blended[:, 1:-1, 1:-1, 1:])  42.9 us
    mul x32, local copies, waits for them, and re-layouts, divergence(): along_third * (blended[:, 1:-1, 1:-1, :-1] - blended[:, 1:-1, 1:-1, 1:])  24.5 us
    mul x32, local copies, waits for them, and re-layouts, divergence(): along_second * (blended[:, 1:-1, :-1, 1:-1] - blended[:, 1:-1, 1:, 1:-1])  24.3 us
    slice x2, local copies, waits for them, and re-layouts, on_device(): shaped[:, :local_solution].reshape((groups * local_solution,) + trailing)  23.7 us
  transfers between devices with their start and end apart: 3, of which 3 were waited for; matrix products, arithmetic and copies ran while one was open for 0% of the time, Pallas kernels for 0%

commit v1 on v0

--- a/solution.py
+++ b/solution.py
@@ -69,7 +69,9 @@
     padding = ((0, 0), (0, 0), (1, 1), (1, 1))
     stacked = jnp.concatenate([solution_modes, coefficient_modes], axis=0)
     rimmed = with_halo(stacked, (("tiles", 1),), 1)
-    everyone = lax.all_gather(rimmed, "modes", axis=0, tiled=True)
+    everyone = jnp.concatenate(
+        lax.all_to_all(jnp.stack([rimmed] * lax.axis_size("modes")), "modes", 0, 0), axis=0
+    )
     trailing = everyone.shape[1:]
     shaped = everyone.reshape((groups, local_solution + local_coefficient) + trailing)
     all_solution = shaped[:, :local_solution].reshape((groups * local_solution,) + trailing)

time: 710 us -> 850 us (1.20)
  the two profiles are of different devices: /device:TPU:1 before, /device:TPU:73 now
where the time goes in v1:
time: 850 us; the launch traced here: 839 us
  waiting for transfers between devices  220 us (26%)
  local copies, waits for them, and re-layouts  187 us (22%)
  other arithmetic  160 us (19%)
  loops' own time  152 us (18%)
  matrix products  106 us (12%)
  starting transfers between devices  13.7 us (2%)
    all_to_all x1, waiting for transfers between devices, on_device(): lax.all_to_all(jnp.stack([rimmed] * lax.axis_size('modes')), 'modes', 0, 0)  211 us
    another operation x1, loops' own time, block_output(): lax.scan(advance, start, jnp.arange(source_rows.shape[0], dtype=jnp.int32))  152 us
    dot_general x32, matrix products, slot_term(): jnp.einsum('ij,jxyz->ixyz', block_matrix, source_modes, precision=lax.Pre...  106 us
    add x32, other arithmetic, advance(): return (running + term, None)  84.7 us
    mul x32, other arithmetic, divergence(): along_third * (blended[:, 1:-1, 1:-1, :-1] - blended[:, 1:-1, 1:-1, 1:])  43 us
    mul x32, local copies, waits for them, and re-layouts, divergence(): along_third * (blended[:, 1:-1, 1:-1, :-1] - blended[:, 1:-1, 1:-1, 1:])  24.5 us
    mul x32, local copies, waits for them, and re-layouts, divergence(): along_second * (blended[:, 1:-1, :-1, 1:-1] - blended[:, 1:-1, 1:, 1:-1])  24.3 us
    slice x2, local copies, waits for them, and re-layouts, on_device(): shaped[:, :local_solution].reshape((groups * local_solution,) + trailing)  23.7 us
  transfers between devices with their start and end apart: 3, of which 3 were waited for; matrix products, arithmetic and copies ran while one was open for 0% of the time, Pallas kernels for 0%

profile of v1, /device:TPU:73, one launch (start us, length us, event | category | flops | bytes accessed | tf_op | source)
XLA Modules:
  0.0 839.1 jit_solution(17193200246665808145)
XLA Ops:
  2.0 3.5 collective-permute-start.1
  9.0 6.8 collective-permute-done
  15.9 7.0 stack.2
  22.9 8.3 all-to-all-start
  31.2 211.2 %all-to-all-done = f32[16,40,6,8,128]{4,3,2,1,0:T(8,128)} async-done(((f32[16,40,6,8,128]{4,3,2,1,0:T(8,128)}), f32[16,40,6,8,128]{4,3,2,1,0:T(8,128)}, u32[]{:S(2)}, u32[]{:S(2)}) %all-to-all-start) | async-done | bytes 15728672 | tf_op jit(solution)/shard_map/all_to_all | solution.py:73
  252.3 10.5 %slice.107 = f32[16,32,6,8,128]{4,3,2,1,0:T(8,128)} slice(f32[16,40,6,8,128]{4,3,2,1,0:T(8,128)} %all-to-all-done), slice={[0:16], [0:32], [0:6], [0:8], [0:128]} | slice | bytes 25165824 | tf_op jit(solution)/shard_map/slice | solution.py:77
  262.8 13.2 %copy.6 = f32[16,32,6,8,128]{4,1,0,3,2:T(8,128)} copy(f32[16,32,6,8,128]{4,3,2,1,0:T(8,128)} %slice.107) | data formatting | bytes 25165824 | tf_op jit(solution)/shard_map/slice | solution.py:77
  276.0 15.0 %pad.8 = f32[512,6,10,130]{3,0,2,1:T(8,128)} pad(f32[512,6,8,128]{3,0,2,1:T(8,128)} %bitcast.38, f32[]{:T(128)} %constant.32.clone.1), padding=0_0x0_0x1_1x1_1 | pad | bytes 28557316 | tf_op jit(solution)/shard_map/jit(_pad)/pad | solution.py:79
  291.0 545.9 %while.11 = (s32[]{:T(128)}, f32[32,4,8,128]{3,0,2,1:T(8,128)}, s32[32]{0:T(128)S(1)}, s32[32]{0:T(128)S(1)}, f32[128,5,8,128]{3,2,1,0:T(8,128)}, /*index=5*/f32...) while((s32[]{:T(128)}, f32[32,4,8,128]{3,0,2,1:T(8,128)}, ...), condition=%wide.region_1.2_spmd.clone, body=%wide.region_0.1_spmd.clone.sunk | while | flops 97650696 | bytes 12662481 | solution.py:60
  312.0 3.3 fusion.24
  363.2 3.3 fusion.24
  380.2 3.3 fusion.24
  397.3 3.3 fusion.24
  448.5 3.3 fusion.24
  499.7 3.3 fusion.24
  516.7 3.3 fusion.24
  533.8 3.3 fusion.24
  585.0 3.3 fusion.24
  602.0 3.3 fusion.24
  636.2 3.3 fusion.24
  653.2 3.3 fusion.24
  704.4 3.3 fusion.24
  721.5 3.3 fusion.24
  789.7 3.3 fusion.24
  (354 shorter events, 361.4 us)
Async XLA Ops:
  2.0 7.0 collective-permute-start.1
  5.5 10.3 %collective-permute-start = (f32[40,1,8,128]{3,2,1,0:T(8,128)S(1)}, f32[40,1,8,128]{3,2,1,0:T(8,128)S(1)}, u32[]{:S(2)}, u32[]{:S(2)}) collective-permute-start(f32[40,1,8,128]{3,2,1,0:T(8,128)S(1)} %get-tuple-element.111), channel_id=1, source_target_pairs={{0,1},{1,2},{2,3},{3,4},{4,5},{5,6},{6,7},{8,9},{9,10},{10,11},{11... | collective-permute-start | bytes 491528 | tf_op jit(solution)/shard_map/ppermute | solution.py:14
  22.9 219.5 %all-to-all-start = ((f32[16,40,6,8,128]{4,3,2,1,0:T(8,128)}), f32[16,40,6,8,128]{4,3,2,1,0:T(8,128)}, u32[]{:S(2)}, u32[]{:S(2)}) async-start(f32[16,40,6,8,128]{4,3,2,1,0:T(8,128)} %stack.2), calls=%async_computation | async-start | bytes 31457280 | tf_op jit(solution)/shard_map/all_to_all | solution.py:73
  276.0 15.0 %copy-start = (s32[1,32]{1,0:T(1,128)S(1)}, s32[1,32]{1,0:T(1,128)}, u32[]{:S(2)}) copy-start(s32[1,32]{1,0:T(1,128)} %param.11) | copy-start | bytes 388
  276.0 15.0 %copy-start.1 = (s32[1,32]{1,0:T(1,128)S(1)}, s32[1,32]{1,0:T(1,128)}, u32[]{:S(2)}) copy-start(s32[1,32]{1,0:T(1,128)} %param.10) | copy-start | bytes 388
